TPU v7x, 256 devices: a whole 4x4x8 slice. The times are simulated.
256 devices in a mesh: tx: 4 (over y), ty: 2 (over z_lo), ea: 32 (over z_hi, x, core).
Axes of the slice: x: 4, y: 4, z: 8 (z_hi: 4, z_lo: 2; z = z_hi * 2 + z_lo), core: 2. Of those that a mesh axis runs over, the one named last changes fastest.
Arguments:
- science: float32 [32, 512, 512], P('ea', 'tx', 'ty'), may hold values from -6 to 6
- inv_variance: float32 [32, 512, 512], P('ea', 'tx', 'ty'), may hold values from 0.25 to 4
- psf_taps: float32 [32, 9], P('ea'), may hold values from 0.05 to 1
- epoch_times: int32 [32], replicated, may hold values from 0 to 256, as said below
- velocities: int32 [192, 2], P('ea'), may hold values from -15 to 15
Outputs:
- likelihood: float32 [192, 512, 512], P('ea', 'tx', 'ty')
Inputs may be any that keep to these rules, and one draw needn't show every extreme that they name: `epoch_times`: the first epoch has time 0 and the last has time 256.
All inputs are finite; a program needn't handle non-finite values.
Results may differ from a plain program's by a relative error of at most 0.0053.
Values may be sent and summed in bfloat16 or wider, within the bound.
A program may use at most 64 MiB of HBM per device.

v0:
```python
import jax
import jax.numpy as jnp
from jax import lax
from jax.sharding import PartitionSpec as P

REACH = 32
PR = 4


def extended(cells, sides, width):
    for axis, dim in sides:
        count = lax.axis_size(axis)
        ends = count - 1
        head = lax.slice_in_dim(cells, 0, width, axis=dim)
        tail = lax.slice_in_dim(cells, cells.shape[dim] - width, cells.shape[dim], axis=dim)
        cells = jnp.concatenate(
            [
                lax.ppermute(tail, axis, [(i, (i + 1) % count) for i in range(ends)]),
                cells,
                lax.ppermute(head, axis, [((i + 1) % count, i) for i in range(ends)]),
            ],
            axis=dim,
        )
    return cells


def blur(field, kern):
    count = kern.shape[1]
    rows = field.shape[1] - count + 1
    acc = kern[:, 0, None, None] * field[:, 0:rows, :]
    for k in range(1, count):
        acc = acc + kern[:, k, None, None] * field[:, k : k + rows, :]
    cols = acc.shape[2] - count + 1
    out = kern[:, 0, None, None] * acc[:, :, 0:cols]
    for k in range(1, count):
        out = out + kern[:, k, None, None] * acc[:, :, k : k + cols]
    return out


def spline_taps(speed, tvals):
    moved = jnp.floor_divide(speed * tvals, 8)
    whole = jnp.floor_divide(moved, 16)
    frac = (moved - 16 * whole).astype(jnp.float32) / 16.0
    frac2 = frac * frac
    frac3 = frac2 * frac
    weights = jnp.stack(
        [
            (1.0 - frac) ** 3 / 6.0,
            (3.0 * frac3 - 6.0 * frac2 + 4.0) / 6.0,
            (-3.0 * frac3 + 3.0 * frac2 + 3.0 * frac + 1.0) / 6.0,
            frac3 / 6.0,
        ],
        -1,
    )
    return (whole, weights.astype(jnp.bfloat16))


def band_matrix(whole, weights, count, span):
    target = lax.broadcasted_iota(jnp.int32, (1, count, span), 2)
    source = lax.broadcasted_iota(jnp.int32, (1, count, span), 1)
    offset = target - source - (REACH + whole - 1)[:, None, None]
    matrix = jnp.zeros((whole.shape[0], count, span), jnp.bfloat16)
    for a in range(4):
        matrix = matrix + jnp.where(
            offset == a, weights[:, a, None, None], jnp.zeros((), jnp.bfloat16)
        )
    return matrix


def stack_block(padded, tvals, velocities, out_rows, out_cols):
    pad_rows = padded.shape[2]
    pad_cols = padded.shape[3]

    def one_hyp(speed):
        whole_r, w_r = spline_taps(speed[0], tvals)
        whole_c, w_c = spline_taps(speed[1], tvals)
        row_band = band_matrix(whole_r, w_r, out_rows, pad_rows)
        col_band = band_matrix(whole_c, w_c, out_cols, pad_cols)
        moved_rows = jnp.einsum(
            "erp,eipk->eirk", row_band, padded, preferred_element_type=jnp.float32
        ).astype(jnp.bfloat16)
        return jnp.einsum("eirk,eck->irc", moved_rows, col_band, preferred_element_type=jnp.float32)

    return lax.map(one_hyp, velocities)


def shards(science, inv_variance, psf_taps, epoch_times, velocities):
    out_rows = science.shape[1]
    out_cols = science.shape[2]
    kern_p = psf_taps / jnp.sum(psf_taps, axis=1, keepdims=True)
    kern_q = kern_p * kern_p
    raw_pair = jnp.stack([science * inv_variance, inv_variance], 0)
    framed = extended(raw_pair, (("tx", 2), ("ty", 3)), PR)
    psi = blur(framed[0], kern_p).astype(jnp.bfloat16)
    phi = blur(framed[1], kern_q).astype(jnp.bfloat16)
    images = jnp.stack([psi, phi], 1)
    every_epoch = lax.all_gather(images, "ea", axis=0, tiled=True)
    padded = extended(every_epoch, (("tx", 2), ("ty", 3)), REACH)
    stacks = stack_block(padded, epoch_times, velocities, out_rows, out_cols)
    return stacks[:, 0] / jnp.sqrt(stacks[:, 1])


def solution(mesh):
    in_specs = (P("ea", "tx", "ty"), P("ea", "tx", "ty"), P("ea", None), P(), P("ea", None))
    out_specs = P("ea", "tx", "ty")
    return jax.shard_map(shards, mesh=mesh, in_specs=in_specs, out_specs=out_specs, check_vma=False)
```

profile of v0, /device:TPU:8, one launch (start us, length us, event | category | flops | bytes accessed | tf_op | source)
XLA Modules:
  0.0 320.8 jit_solution(10306133424879456887)
XLA Ops:
  8.2 3.5 %collective-permute-start = (f32[2,1,4,256]{3,2,1,0:T(4,128)S(1)}, f32[2,1,4,256]{3,2,1,0:T(4,128)S(1)}, u32[]{:S(2)}, u32[]{:S(2)}) collective-permute-start(f32[2,1,4,256]{3,2,1,0:T(4,128)S(1)} %get-tuple-element.184), channel_id=1, source_target_pairs={{0,64},{64,128},{128,192},{1,65},{65,129},{129,193},{2,66},{66,130... | collective-permute-start | bytes 24584 | tf_op jit(solution)/shard_map/ppermute | solution.py:18
  18.3 3.8 %collective-permute-start.2 = (f32[2,1,136,4]{3,2,1,0:T(8,128)S(1)}, f32[2,1,136,4]{3,2,1,0:T(8,128)S(1)}, u32[]{:S(2)}, u32[]{:S(2)}) collective-permute-start(f32[2,1,136,4]{3,2,1,0:T(8,128)S(1)} %get-tuple-element.182), channel_id=1, source_target_pairs={{0,32},{1,33},{2,34},{3,35},{4,36},{5,37},{6,38},{7,39},{8,40},{9,... | collective-permute-start | bytes 13064 | tf_op jit(solution)/shard_map/ppermute | solution.py:18
  24.7 4.4 %collective-permute-done.3 = f32[2,1,136,4]{3,2,1,0:T(8,128)S(1)} collective-permute-done((f32[2,1,136,4]{3,2,1,0:T(8,128)S(1)}, f32[2,1,136,4]{3,2,1,0:T(8,128)S(1)}, u32[]{:S(2)}, u32[]{:S(2)}) %collective-permute-start.3) | collective-permute-done | bytes 4384 | tf_op jit(solution)/shard_map/ppermute | solution.py:20
  30.3 6.0 %fusion.111 = f32[1,128,264]{2,1,0:T(8,128)S(1)} fusion(f32[1,136,264]{2,1,0:T(8,128)S(1)} %get-tuple-element.180, f32[]{:T(128)} %bitcast.29, f32[]{:T(128)} %bitcast.28, f32[]{:T(128)} %bitcast.27, f32[]{:T(128)} %bitcast.26, f32[]{:T(128)} %bitcast.25, f32[]{:T(128)} %bitcast.24, f32[]{:T(128)} %bitcast.23, f32[]{:T(128)} %bitcast.22, f32[]{:T(128)} %bitcast.18), kind=kLoop, calls=%fused_computation.141 | loop fusion | flops 574464 | bytes 1351716 | tf_op jit(solution)/shard_map/add | solution.py:32
  36.3 6.2 %fusion.137 = bf16[1,1,128,256]{3,2,1,0:T(8,128)(2,1)S(1)} fusion(f32[1,128,264]{2,1,0:T(8,128)S(1)} %fusion.111, f32[]{:T(128)} %bitcast.29, f32[]{:T(128)} %bitcast.28, f32[]{:T(128)} %bitcast.27, f32[]{:T(128)} %bitcast.26, f32[]{:T(128)} %bitcast.25, f32[]{:T(128)} %bitcast.24, f32[]{:T(128)} %bitcast.23, f32[]{:T(128)} %bitcast.22, f32[]{:T(128)} %bitcast.18), kind=kLoop, calls=%fused_computation.195 | loop fusion | flops 589824 | bytes 1245220 | tf_op jit(solution)/shard_map/stack | solution.py:96
  42.4 5.7 %fusion.103 = f32[1,128,264]{2,1,0:T(8,128)S(1)} fusion(f32[1,136,264]{2,1,0:T(8,128)S(1)} %get-tuple-element.181, f32[]{:T(128)} %bitcast.40, f32[]{:T(128)} %bitcast.39, f32[]{:T(128)} %bitcast.38, f32[]{:T(128)} %bitcast.37, f32[]{:T(128)} %bitcast.36, f32[]{:T(128)} %bitcast.35, f32[]{:T(128)} %bitcast.34, f32[]{:T(128)} %bitcast.33, f32[]{:T(128)} %bitcast.31), kind=kLoop, calls=%fused_computation.124 | loop fusion | flops 574464 | bytes 1351716 | tf_op jit(solution)/shard_map/add | solution.py:32
  48.2 5.9 %fusion.138 = bf16[1,1,128,256]{3,2,1,0:T(8,128)(2,1)S(1)} fusion(f32[1,128,264]{2,1,0:T(8,128)S(1)} %fusion.103, f32[]{:T(128)} %bitcast.40, f32[]{:T(128)} %bitcast.39, f32[]{:T(128)} %bitcast.38, f32[]{:T(128)} %bitcast.37, f32[]{:T(128)} %bitcast.36, f32[]{:T(128)} %bitcast.35, f32[]{:T(128)} %bitcast.34, f32[]{:T(128)} %bitcast.33, f32[]{:T(128)} %bitcast.31), kind=kLoop, calls=%fused_computation.196 | loop fusion | flops 589824 | bytes 1245220 | tf_op jit(solution)/shard_map/stack | solution.py:96
  54.7 62.2 %all-gather.2.cloned.1.call-done = bf16[32,2,128,256]{3,2,1,0:T(8,128)(2,1)} async-done(((bf16[1,2,128,256]{3,2,1,0:T(8,128)(2,1)}), bf16[32,2,128,256]{3,2,1,0:T(8,128)(2,1)}) %all-gather.2.cloned.1.call-update) | async-done | bytes 4194320 | tf_op jit(solution)/shard_map/all_gather | solution.py:97
  118.8 3.4 %collective-permute-start.4 = (bf16[32,2,32,256]{3,2,1,0:T(8,128)(2,1)S(1)}, bf16[32,2,32,256]{3,2,1,0:T(8,128)(2,1)S(1)}, u32[]{:S(2)}, u32[]{:S(2)}) collective-permute-start(bf16[32,2,32,256]{3,2,1,0:T(8,128)(2,1)S(1)} %get-tuple-element.179), channel_id=1, source_target_pairs={{0,64},{64,128},{128,192},{1,65},{65,129},{129,193},{2,66},{66,130... | collective-permute-start | bytes 3145736 | tf_op jit(solution)/shard_map/ppermute | solution.py:18
  124.7 21.3 %collective-permute-done.4 = bf16[32,2,32,256]{3,2,1,0:T(8,128)(2,1)S(1)} collective-permute-done((bf16[32,2,32,256]{3,2,1,0:T(8,128)(2,1)S(1)}, bf16[32,2,32,256]{3,2,1,0:T(8,128)(2,1)S(1)}, u32[]{:S(2)}, u32[]{:S(2)}) %collective-permute-start.4) | collective-permute-done | bytes 1048608 | tf_op jit(solution)/shard_map/ppermute | solution.py:18
  149.2 3.7 %fusion.141 = (bf16[32,2,192,32]{3,2,1,0:T(8,128)(2,1)}, bf16[32,2,192,32]{3,2,1,0:T(8,128)(2,1)S(1)}) fusion(bf16[32,2,192,256]{3,2,1,0:T(8,128)(2,1)S(1)} %constant_dynamic-update-slice_fusion), kind=kLoop, calls=%fused_computation.205 | loop fusion | bytes 3145728 | tf_op jit(solution)/shard_map/slice | solution.py:15
  152.9 4.1 %copy.8 = bf16[32,2,192,32]{2,3,1,0:T(8,128)(2,1)} copy(bf16[32,2,192,32]{3,2,1,0:T(8,128)(2,1)} %get-tuple-element.176) | data formatting | bytes 1572864 | tf_op jit(solution)/shard_map/slice | solution.py:15
  157.0 3.4 %collective-permute-start.6 = (bf16[32,2,192,32]{2,3,1,0:T(8,128)(2,1)}, bf16[32,2,192,32]{2,3,1,0:T(8,128)(2,1)}, u32[]{:S(2)}, u32[]{:S(2)}) collective-permute-start(bf16[32,2,192,32]{2,3,1,0:T(8,128)(2,1)} %copy.8), channel_id=1, source_target_pairs={{0,32},{1,33},{2,34},{3,35},{4,36},{5,37},{6,38},{7,39},{8,40},{9,... | collective-permute-start | bytes 2359304 | tf_op jit(solution)/shard_map/ppermute | solution.py:18
  160.4 3.0 copy.9
  164.9 16.5 %collective-permute-done.6 = bf16[32,2,192,32]{2,3,1,0:T(8,128)(2,1)} collective-permute-done((bf16[32,2,192,32]{2,3,1,0:T(8,128)(2,1)}, bf16[32,2,192,32]{2,3,1,0:T(8,128)(2,1)}, u32[]{:S(2)}, u32[]{:S(2)}) %collective-permute-start.6) | collective-permute-done | bytes 786464 | tf_op jit(solution)/shard_map/ppermute | solution.py:18
  181.4 3.4 %copy.10 = bf16[32,2,192,32]{3,2,1,0:T(8,128)(2,1)S(1)} copy(bf16[32,2,192,32]{2,3,1,0:T(8,128)(2,1)} %collective-permute-done.6) | data formatting | bytes 1572864 | tf_op jit(solution)/shard_map/ppermute | solution.py:18
  184.8 4.7 %collective-permute-done.7 = bf16[32,2,192,32]{2,3,1,0:T(8,128)(2,1)} collective-permute-done((bf16[32,2,192,32]{2,3,1,0:T(8,128)(2,1)}, bf16[32,2,192,32]{2,3,1,0:T(8,128)(2,1)}, u32[]{:S(2)}, u32[]{:S(2)}) %collective-permute-start.7) | collective-permute-done | bytes 786464 | tf_op jit(solution)/shard_map/ppermute | solution.py:20
  189.5 3.9 %copy.11 = bf16[32,2,192,32]{3,2,1,0:T(8,128)(2,1)} copy(bf16[32,2,192,32]{2,3,1,0:T(8,128)(2,1)} %collective-permute-done.7) | data formatting | bytes 1572864 | tf_op jit(solution)/shard_map/ppermute | solution.py:20
  193.4 11.6 %pad_maximum_fusion = bf16[32,2,192,320]{3,2,1,0:T(8,128)(2,1)} fusion(bf16[32,2,192,32]{3,2,1,0:T(8,128)(2,1)} %copy.11, bf16[32,2,192,256]{3,2,1,0:T(8,128)(2,1)} %copy-done, bf16[32,2,192,32]{3,2,1,0:T(8,128)(2,1)S(1)} %copy.10), kind=kLoop, calls=%fused_computation.117 | loop fusion | flops 23592960 | bytes 15728640 | tf_op jit(solution)/shard_map/concatenate | solution.py:16
  205.0 106.6 %while.15 = (s32[]{:T(128)}, f32[6,2,128,256]{3,2,0,1:T(8,128)}, s32[6,2]{0,1:T(2,128)S(1)}, s32[32]{0:T(128)S(1)}, bf16[32,2,192,320]{3,2,1,0:T(8,128)(2,1)}, /*index=5*/s32[]{:T(128)}) while((s32[]{:T(128)}, f32[6,2,128,256]{3,2,0,1:T(8,128)}, s32[6,2]{0,1:T(2,128)S(1)}, s32[32]{0:T(128)S(1)}, bf16[32,2,192,320]{3,2,1,0:T(8,128)(2,1)}, ...), condition=%wide.region_2.3_spmd, body=%wide.region_1.2_spmd.sunk | while | flops 2396370688 | bytes 19467128 | solution.py:84
  208.3 7.6 %fusion.178 = bf16[32,2,128,320]{2,3,0,1:T(8,128)(2,1)S(1)} fusion(bf16[32,2,192,320]{3,2,1,0:T(8,128)(2,1)} %get-tuple-element.288, s32[32]{0:T(128)S(1)} %get-tuple-element.267, s32[128,192]{1,0:T(8,128)S(1)} %iota_subtract_fusion.5, bf16[32]{0:T(256)(128)(2,1)S(1)} %get-tuple-element.268, ...), kind=kOutput, calls=%fused_computation.19.clone.clone.clone.clone.clone.2.clone.1 | convolution fusion | flops 1022623744 | bytes 13205888 | tf_op jit(solution)/shard_map/while/body/eval_jaxpr/erp,eipk->eirk/dot_general | solution.py:79
  215.9 6.9 %fusion.179 = f32[6,2,128,256]{3,2,0,1:T(8,128)} fusion(f32[6,2,128,256]{3,2,0,1:T(8,128)} %get-tuple-element.279, s32[]{:T(128)} %get-tuple-element.278, s32[32]{0:T(128)S(1)} %get-tuple-element.260, s32[256,320]{0,1:T(8,128)S(1)} %iota_subtract_fusion.4, bf16[32]{0:T(256)(128)(2,1)S(1)} %get-tuple-element.263, ...), kind=kOutput, calls=%fused_computation.47.clone.3 | convolution fusion | flops 1373634560 | bytes 5833600 | tf_op jit(solution)/shard_map/while/body/eval_jaxpr/eirk,eck->irc/dot_general | solution.py:82
  226.1 7.6 %fusion.178 = bf16[32,2,128,320]{2,3,0,1:T(8,128)(2,1)S(1)} fusion(bf16[32,2,192,320]{3,2,1,0:T(8,128)(2,1)} %get-tuple-element.288, s32[32]{0:T(128)S(1)} %get-tuple-element.267, s32[128,192]{1,0:T(8,128)S(1)} %iota_subtract_fusion.5, bf16[32]{0:T(256)(128)(2,1)S(1)} %get-tuple-element.268, ...), kind=kOutput, calls=%fused_computation.19.clone.clone.clone.clone.clone.2.clone.1 | convolution fusion | flops 1022623744 | bytes 13205888 | tf_op jit(solution)/shard_map/while/body/eval_jaxpr/erp,eipk->eirk/dot_general | solution.py:79
  233.7 6.9 %fusion.179 = f32[6,2,128,256]{3,2,0,1:T(8,128)} fusion(f32[6,2,128,256]{3,2,0,1:T(8,128)} %get-tuple-element.279, s32[]{:T(128)} %get-tuple-element.278, s32[32]{0:T(128)S(1)} %get-tuple-element.260, s32[256,320]{0,1:T(8,128)S(1)} %iota_subtract_fusion.4, bf16[32]{0:T(256)(128)(2,1)S(1)} %get-tuple-element.263, ...), kind=kOutput, calls=%fused_computation.47.clone.3 | convolution fusion | flops 1373634560 | bytes 5833600 | tf_op jit(solution)/shard_map/while/body/eval_jaxpr/eirk,eck->irc/dot_general | solution.py:82
  243.8 7.6 %fusion.178 = bf16[32,2,128,320]{2,3,0,1:T(8,128)(2,1)S(1)} fusion(bf16[32,2,192,320]{3,2,1,0:T(8,128)(2,1)} %get-tuple-element.288, s32[32]{0:T(128)S(1)} %get-tuple-element.267, s32[128,192]{1,0:T(8,128)S(1)} %iota_subtract_fusion.5, bf16[32]{0:T(256)(128)(2,1)S(1)} %get-tuple-element.268, ...), kind=kOutput, calls=%fused_computation.19.clone.clone.clone.clone.clone.2.clone.1 | convolution fusion | flops 1022623744 | bytes 13205888 | tf_op jit(solution)/shard_map/while/body/eval_jaxpr/erp,eipk->eirk/dot_general | solution.py:79
  251.5 6.9 %fusion.179 = f32[6,2,128,256]{3,2,0,1:T(8,128)} fusion(f32[6,2,128,256]{3,2,0,1:T(8,128)} %get-tuple-element.279, s32[]{:T(128)} %get-tuple-element.278, s32[32]{0:T(128)S(1)} %get-tuple-element.260, s32[256,320]{0,1:T(8,128)S(1)} %iota_subtract_fusion.4, bf16[32]{0:T(256)(128)(2,1)S(1)} %get-tuple-element.263, ...), kind=kOutput, calls=%fused_computation.47.clone.3 | convolution fusion | flops 1373634560 | bytes 5833600 | tf_op jit(solution)/shard_map/while/body/eval_jaxpr/eirk,eck->irc/dot_general | solution.py:82
  261.6 7.6 %fusion.178 = bf16[32,2,128,320]{2,3,0,1:T(8,128)(2,1)S(1)} fusion(bf16[32,2,192,320]{3,2,1,0:T(8,128)(2,1)} %get-tuple-element.288, s32[32]{0:T(128)S(1)} %get-tuple-element.267, s32[128,192]{1,0:T(8,128)S(1)} %iota_subtract_fusion.5, bf16[32]{0:T(256)(128)(2,1)S(1)} %get-tuple-element.268, ...), kind=kOutput, calls=%fused_computation.19.clone.clone.clone.clone.clone.2.clone.1 | convolution fusion | flops 1022623744 | bytes 13205888 | tf_op jit(solution)/shard_map/while/body/eval_jaxpr/erp,eipk->eirk/dot_general | solution.py:79
  269.2 6.9 %fusion.179 = f32[6,2,128,256]{3,2,0,1:T(8,128)} fusion(f32[6,2,128,256]{3,2,0,1:T(8,128)} %get-tuple-element.279, s32[]{:T(128)} %get-tuple-element.278, s32[32]{0:T(128)S(1)} %get-tuple-element.260, s32[256,320]{0,1:T(8,128)S(1)} %iota_subtract_fusion.4, bf16[32]{0:T(256)(128)(2,1)S(1)} %get-tuple-element.263, ...), kind=kOutput, calls=%fused_computation.47.clone.3 | convolution fusion | flops 1373634560 | bytes 5833600 | tf_op jit(solution)/shard_map/while/body/eval_jaxpr/eirk,eck->irc/dot_general | solution.py:82
  279.4 7.6 %fusion.178 = bf16[32,2,128,320]{2,3,0,1:T(8,128)(2,1)S(1)} fusion(bf16[32,2,192,320]{3,2,1,0:T(8,128)(2,1)} %get-tuple-element.288, s32[32]{0:T(128)S(1)} %get-tuple-element.267, s32[128,192]{1,0:T(8,128)S(1)} %iota_subtract_fusion.5, bf16[32]{0:T(256)(128)(2,1)S(1)} %get-tuple-element.268, ...), kind=kOutput, calls=%fused_computation.19.clone.clone.clone.clone.clone.2.clone.1 | convolution fusion | flops 1022623744 | bytes 13205888 | tf_op jit(solution)/shard_map/while/body/eval_jaxpr/erp,eipk->eirk/dot_general | solution.py:79
  287.0 6.9 %fusion.179 = f32[6,2,128,256]{3,2,0,1:T(8,128)} fusion(f32[6,2,128,256]{3,2,0,1:T(8,128)} %get-tuple-element.279, s32[]{:T(128)} %get-tuple-element.278, s32[32]{0:T(128)S(1)} %get-tuple-element.260, s32[256,320]{0,1:T(8,128)S(1)} %iota_subtract_fusion.4, bf16[32]{0:T(256)(128)(2,1)S(1)} %get-tuple-element.263, ...), kind=kOutput, calls=%fused_computation.47.clone.3 | convolution fusion | flops 1373634560 | bytes 5833600 | tf_op jit(solution)/shard_map/while/body/eval_jaxpr/eirk,eck->irc/dot_general | solution.py:82
  297.1 7.6 %fusion.178 = bf16[32,2,128,320]{2,3,0,1:T(8,128)(2,1)S(1)} fusion(bf16[32,2,192,320]{3,2,1,0:T(8,128)(2,1)} %get-tuple-element.288, s32[32]{0:T(128)S(1)} %get-tuple-element.267, s32[128,192]{1,0:T(8,128)S(1)} %iota_subtract_fusion.5, bf16[32]{0:T(256)(128)(2,1)S(1)} %get-tuple-element.268, ...), kind=kOutput, calls=%fused_computation.19.clone.clone.clone.clone.clone.2.clone.1 | convolution fusion | flops 1022623744 | bytes 13205888 | tf_op jit(solution)/shard_map/while/body/eval_jaxpr/erp,eipk->eirk/dot_general | solution.py:79
  304.8 6.9 %fusion.179 = f32[6,2,128,256]{3,2,0,1:T(8,128)} fusion(f32[6,2,128,256]{3,2,0,1:T(8,128)} %get-tuple-element.279, s32[]{:T(128)} %get-tuple-element.278, s32[32]{0:T(128)S(1)} %get-tuple-element.260, s32[256,320]{0,1:T(8,128)S(1)} %iota_subtract_fusion.4, bf16[32]{0:T(256)(128)(2,1)S(1)} %get-tuple-element.263, ...), kind=kOutput, calls=%fused_computation.47.clone.3 | convolution fusion | flops 1373634560 | bytes 5833600 | tf_op jit(solution)/shard_map/while/body/eval_jaxpr/eirk,eck->irc/dot_general | solution.py:82
  (76 shorter events, 43.5 us)
Async XLA Ops:
  6.5 110.4 %all-gather.2.cloned.1.call-start = ((), (), s32[]{:S(2)}) async-start(), calls=%async_computation | async-start | bytes 4325376 | tf_op jit(solution)/shard_map/all_gather | solution.py:97
  8.2 8.4 %collective-permute-start = (f32[2,1,4,256]{3,2,1,0:T(4,128)S(1)}, f32[2,1,4,256]{3,2,1,0:T(4,128)S(1)}, u32[]{:S(2)}, u32[]{:S(2)}) collective-permute-start(f32[2,1,4,256]{3,2,1,0:T(4,128)S(1)} %get-tuple-element.184), channel_id=1, source_target_pairs={{0,64},{64,128},{128,192},{1,65},{65,129},{129,193},{2,66},{66,130... | collective-permute-start | bytes 24584 | tf_op jit(solution)/shard_map/ppermute | solution.py:18
  11.7 5.5 %collective-permute-start.1 = (f32[2,1,4,256]{3,2,1,0:T(4,128)S(1)}, f32[2,1,4,256]{3,2,1,0:T(4,128)S(1)}, u32[]{:S(2)}, u32[]{:S(2)}) collective-permute-start(f32[2,1,4,256]{3,2,1,0:T(4,128)S(1)} %get-tuple-element.185), channel_id=1, source_target_pairs={{64,0},{128,64},{192,128},{65,1},{129,65},{193,129},{66,2},{130,66... | collective-permute-start | bytes 24584 | tf_op jit(solution)/shard_map/ppermute | solution.py:20
  18.3 6.4 %collective-permute-start.2 = (f32[2,1,136,4]{3,2,1,0:T(8,128)S(1)}, f32[2,1,136,4]{3,2,1,0:T(8,128)S(1)}, u32[]{:S(2)}, u32[]{:S(2)}) collective-permute-start(f32[2,1,136,4]{3,2,1,0:T(8,128)S(1)} %get-tuple-element.182), channel_id=1, source_target_pairs={{0,32},{1,33},{2,34},{3,35},{4,36},{5,37},{6,38},{7,39},{8,40},{9,... | collective-permute-start | bytes 13064 | tf_op jit(solution)/shard_map/ppermute | solution.py:18
  22.1 6.9 %collective-permute-start.3 = (f32[2,1,136,4]{3,2,1,0:T(8,128)S(1)}, f32[2,1,136,4]{3,2,1,0:T(8,128)S(1)}, u32[]{:S(2)}, u32[]{:S(2)}) collective-permute-start(f32[2,1,136,4]{3,2,1,0:T(8,128)S(1)} %get-tuple-element.183), channel_id=1, source_target_pairs={{32,0},{33,1},{34,2},{35,3},{36,4},{37,5},{38,6},{39,7},{40,8},{41... | collective-permute-start | bytes 13064 | tf_op jit(solution)/shard_map/ppermute | solution.py:20
  116.9 29.2 %copy-start.1 = (bf16[32,2,128,256]{3,2,1,0:T(8,128)(2,1)S(1)}, bf16[32,2,128,256]{3,2,1,0:T(8,128)(2,1)}, u32[]{:S(2)}) copy-start(bf16[32,2,128,256]{3,2,1,0:T(8,128)(2,1)} %all-gather.2.cloned.1.call-done) | copy-start | bytes 12582916
  118.8 27.2 %collective-permute-start.4 = (bf16[32,2,32,256]{3,2,1,0:T(8,128)(2,1)S(1)}, bf16[32,2,32,256]{3,2,1,0:T(8,128)(2,1)S(1)}, u32[]{:S(2)}, u32[]{:S(2)}) collective-permute-start(bf16[32,2,32,256]{3,2,1,0:T(8,128)(2,1)S(1)} %get-tuple-element.179), channel_id=1, source_target_pairs={{0,64},{64,128},{128,192},{1,65},{65,129},{129,193},{2,66},{66,130... | collective-permute-start | bytes 3145736 | tf_op jit(solution)/shard_map/ppermute | solution.py:18
  122.2 26.9 %collective-permute-start.5 = (bf16[32,2,32,256]{3,2,1,0:T(8,128)(2,1)S(1)}, bf16[32,2,32,256]{3,2,1,0:T(8,128)(2,1)S(1)}, u32[]{:S(2)}, u32[]{:S(2)}) collective-permute-start(bf16[32,2,32,256]{3,2,1,0:T(8,128)(2,1)S(1)} %get-tuple-element.178), channel_id=1, source_target_pairs={{64,0},{128,64},{192,128},{65,1},{129,65},{193,129},{66,2},{130,66... | collective-permute-start | bytes 3145736 | tf_op jit(solution)/shard_map/ppermute | solution.py:20
  149.2 3.7 %copy-start = (bf16[32,2,192,256]{3,2,1,0:T(8,128)(2,1)}, bf16[32,2,192,256]{3,2,1,0:T(8,128)(2,1)S(1)}, u32[]{:S(2)}) copy-start(bf16[32,2,192,256]{3,2,1,0:T(8,128)(2,1)S(1)} %constant_dynamic-update-slice_fusion) | copy-start | bytes 18874372
  157.0 24.4 %collective-permute-start.6 = (bf16[32,2,192,32]{2,3,1,0:T(8,128)(2,1)}, bf16[32,2,192,32]{2,3,1,0:T(8,128)(2,1)}, u32[]{:S(2)}, u32[]{:S(2)}) collective-permute-start(bf16[32,2,192,32]{2,3,1,0:T(8,128)(2,1)} %copy.8), channel_id=1, source_target_pairs={{0,32},{1,33},{2,34},{3,35},{4,36},{5,37},{6,38},{7,39},{8,40},{9,... | collective-permute-start | bytes 2359304 | tf_op jit(solution)/shard_map/ppermute | solution.py:18
  163.4 26.1 %collective-permute-start.7 = (bf16[32,2,192,32]{2,3,1,0:T(8,128)(2,1)}, bf16[32,2,192,32]{2,3,1,0:T(8,128)(2,1)}, u32[]{:S(2)}, u32[]{:S(2)}) collective-permute-start(bf16[32,2,192,32]{2,3,1,0:T(8,128)(2,1)} %copy.9), channel_id=1, source_target_pairs={{32,0},{33,1},{34,2},{35,3},{36,4},{37,5},{38,6},{39,7},{40,8},{41... | collective-permute-start | bytes 2359304 | tf_op jit(solution)/shard_map/ppermute | solution.py:20
  193.4 11.6 %copy-start.2 = (s32[32]{0:T(128)S(1)}, s32[32]{0:T(128)}, u32[]{:S(2)}) copy-start(s32[32]{0:T(128)} %param.10) | copy-start | bytes 388
  193.4 11.6 %copy-start.3 = (s32[6,2]{0,1:T(2,128)S(1)}, s32[6,2]{0,1:T(2,128)}, u32[]{:S(2)}) copy-start(s32[6,2]{0,1:T(2,128)} %param.11) | copy-start | bytes 148
Sparse Core Ops, SparseCore 0:
  54.8 61.9 all-gather.1
where the time goes:
time: 322 us; the launch traced here: 321 us
  waiting for transfers between devices  113 us (35%)
  matrix products  86.9 us (27%)
  other arithmetic  60.5 us (19%)
  local copies, waits for them, and re-layouts  25 us (8%)
  starting transfers between devices  21.7 us (7%)
  between operations  13.6 us (4%)
    all_gather x1, waiting for transfers between devices, shards(): every_epoch = lax.all_gather(images, 'ea', axis=0, tiled=True)  62.2 us
    dot_general x6, matrix products, one_hyp(): jnp.einsum('erp,eipk->eirk', row_band, padded, preferred_element_type=jnp...  45.7 us
    dot_general x6, matrix products, one_hyp(): jnp.einsum('eirk,eck->irc', moved_rows, col_band, preferred_element_type=...  41.3 us
    ppermute x4, waiting for transfers between devices, extended(): lax.ppermute(tail, axis, [(i, (i + 1) % count) for i in range(ends)])  38.4 us
    ppermute x4, starting transfers between devices, extended(): lax.ppermute(tail, axis, [(i, (i + 1) % count) for i in range(ends)])  14.1 us
    concatenate x3, other arithmetic, extended(): jnp.concatenate([lax.ppermute(tail, axis, [(i, (i + 1) % count) for i in...  13.7 us
    another operation x3, other arithmetic, shards(): images = jnp.stack([psi, phi], 1)  12.7 us
    ppermute x4, waiting for transfers between devices, extended(): lax.ppermute(head, axis, [((i + 1) % count, i) for i in range(ends)])  12.4 us
  transfers between devices with their start and end apart: 9, of which 8 were waited for; matrix products, arithmetic and copies ran while one was open for 3% of the time, Pallas kernels for 0%

commit v1 on v0

--- a/solution.py
+++ b/solution.py
@@ -94,7 +94,9 @@
     psi = blur(framed[0], kern_p).astype(jnp.bfloat16)
     phi = blur(framed[1], kern_q).astype(jnp.bfloat16)
     images = jnp.stack([psi, phi], 1)
-    every_epoch = lax.all_gather(images, "ea", axis=0, tiled=True)
+    every_epoch = jnp.concatenate(
+        lax.all_to_all(jnp.stack([images] * lax.axis_size("ea")), "ea", 0, 0), axis=0
+    )
     padded = extended(every_epoch, (("tx", 2), ("ty", 3)), REACH)
     stacks = stack_block(padded, epoch_times, velocities, out_rows, out_cols)
     return stacks[:, 0] / jnp.sqrt(stacks[:, 1])

time: 322 us -> 353 us (1.096)
  blocking collectives: 0 us -> 106 us
  waiting for transfers between devices: 113 us -> 50.3 us
  between operations: 13.6 us -> 0.17 us
    all_to_all x0 -> x1, blocking collectives: none -> 106 us  [shards(): lax.all_to_all(jnp.stack([images] * lax.axis_size('ea')), 'ea', 0, 0)]
    all_gather x1 -> x0, waiting for transfers between devices: 62.2 us -> none  [shards(): every_epoch = lax.all_gather(images, 'ea', axis=0, tiled=True)]
    concatenate x3 -> x4, other arithmetic: 13.7 us -> 17.8 us  [extended(): jnp.concatenate([lax.ppermute(tail, axis, [(i, (i + 1) % count) for i in...]
    slice x3 -> x4, local copies, waits for them, and re-layouts: 7.89 us -> 7.61 us  [extended(): lax.slice_in_dim(cells, cells.shape[dim] - width, cells.shape[dim], axis=...]
  transfers between devices with their start and end apart: 9 -> 8, of which waited for: 8 -> 7; matrix products, arithmetic and copies ran while one was open for 3% -> 3% of each run, Pallas kernels for 0% -> 0%
where the time goes in v1:
time: 353 us; the launch traced here: 351 us
  blocking collectives  106 us (30%)
  matrix products  86.9 us (25%)
  other arithmetic  63.1 us (18%)
  waiting for transfers between devices  50.3 us (14%)
  local copies, waits for them, and re-layouts  23.7 us (7%)
  starting transfers between devices  20.6 us (6%)
    all_to_all x1, blocking collectives, shards(): lax.all_to_all(jnp.stack([images] * lax.axis_size('ea')), 'ea', 0, 0)  106 us
    dot_general x6, matrix products, one_hyp(): jnp.einsum('erp,eipk->eirk', row_band, padded, preferred_element_type=jnp...  45.6 us
    dot_general x6, matrix products, one_hyp(): jnp.einsum('eirk,eck->irc', moved_rows, col_band, preferred_element_type=...  41.2 us
    ppermute x4, waiting for transfers between devices, extended(): lax.ppermute(tail, axis, [(i, (i + 1) % count) for i in range(ends)])  37.8 us
    concatenate x4, other arithmetic, extended(): jnp.concatenate([lax.ppermute(tail, axis, [(i, (i + 1) % count) for i in...  17.8 us
    ppermute x4, starting transfers between devices, extended(): lax.ppermute(tail, axis, [(i, (i + 1) % count) for i in range(ends)])  12.7 us
    ppermute x4, waiting for transfers between devices, extended(): lax.ppermute(head, axis, [((i + 1) % count, i) for i in range(ends)])  12.6 us
    another operation x3, other arithmetic, shards(): images = jnp.stack([psi, phi], 1)  12 us
  transfers between devices with their start and end apart: 8, of which 7 were waited for; matrix products, arithmetic and copies ran while one was open for 3% of the time, Pallas kernels for 0%

profile of v1, /device:TPU:8, one launch (start us, length us, event | category | flops | bytes accessed | tf_op | source)
XLA Modules:
  0.0 351.3 jit_solution(2062053520824853920)
XLA Ops:
  1.7 3.5 collective-permute-start
  11.8 3.8 %collective-permute-start.2 = (f32[2,1,136,4]{3,2,1,0:T(8,128)S(1)}, f32[2,1,136,4]{3,2,1,0:T(8,128)S(1)}, u32[]{:S(2)}, u32[]{:S(2)}) collective-permute-start(f32[2,1,136,4]{3,2,1,0:T(8,128)S(1)} %get-tuple-element.182), channel_id=1, source_target_pairs={{0,32},{1,33},{2,34},{3,35},{4,36},{5,37},{6,38},{7,39},{8,40},{9,... | collective-permute-start | bytes 13064 | tf_op jit(solution)/shard_map/ppermute | solution.py:18
  18.2 4.4 %collective-permute-done.3 = f32[2,1,136,4]{3,2,1,0:T(8,128)S(1)} collective-permute-done((f32[2,1,136,4]{3,2,1,0:T(8,128)S(1)}, f32[2,1,136,4]{3,2,1,0:T(8,128)S(1)}, u32[]{:S(2)}, u32[]{:S(2)}) %collective-permute-start.3) | collective-permute-done | bytes 4384 | tf_op jit(solution)/shard_map/ppermute | solution.py:20
  23.7 6.0 %fusion.111 = f32[1,128,264]{2,1,0:T(8,128)S(1)} fusion(f32[1,136,264]{2,1,0:T(8,128)S(1)} %get-tuple-element.180, f32[]{:T(128)} %bitcast.29, f32[]{:T(128)} %bitcast.28, f32[]{:T(128)} %bitcast.27, f32[]{:T(128)} %bitcast.26, f32[]{:T(128)} %bitcast.25, f32[]{:T(128)} %bitcast.24, f32[]{:T(128)} %bitcast.23, f32[]{:T(128)} %bitcast.22, f32[]{:T(128)} %bitcast.18), kind=kLoop, calls=%fused_computation.142 | loop fusion | flops 574464 | bytes 1351716 | tf_op jit(solution)/shard_map/add | solution.py:32
  29.7 6.1 %fusion.137 = bf16[1,1,128,256]{3,2,1,0:T(8,128)(2,1)S(1)} fusion(f32[1,128,264]{2,1,0:T(8,128)S(1)} %fusion.111, f32[]{:T(128)} %bitcast.29, f32[]{:T(128)} %bitcast.28, f32[]{:T(128)} %bitcast.27, f32[]{:T(128)} %bitcast.26, f32[]{:T(128)} %bitcast.25, f32[]{:T(128)} %bitcast.24, f32[]{:T(128)} %bitcast.23, f32[]{:T(128)} %bitcast.22, f32[]{:T(128)} %bitcast.18), kind=kLoop, calls=%fused_computation.196 | loop fusion | flops 589824 | bytes 1245220 | tf_op jit(solution)/shard_map/stack | solution.py:96
  35.8 5.8 %fusion.103 = f32[1,128,264]{2,1,0:T(8,128)S(1)} fusion(f32[1,136,264]{2,1,0:T(8,128)S(1)} %get-tuple-element.181, f32[]{:T(128)} %bitcast.40, f32[]{:T(128)} %bitcast.39, f32[]{:T(128)} %bitcast.38, f32[]{:T(128)} %bitcast.37, f32[]{:T(128)} %bitcast.36, f32[]{:T(128)} %bitcast.35, f32[]{:T(128)} %bitcast.34, f32[]{:T(128)} %bitcast.33, f32[]{:T(128)} %bitcast.31), kind=kLoop, calls=%fused_computation.125 | loop fusion | flops 574464 | bytes 1351716 | tf_op jit(solution)/shard_map/add | solution.py:32
  41.6 5.9 %fusion.138 = bf16[1,1,128,256]{3,2,1,0:T(8,128)(2,1)S(1)} fusion(f32[1,128,264]{2,1,0:T(8,128)S(1)} %fusion.103, f32[]{:T(128)} %bitcast.40, f32[]{:T(128)} %bitcast.39, f32[]{:T(128)} %bitcast.38, f32[]{:T(128)} %bitcast.37, f32[]{:T(128)} %bitcast.36, f32[]{:T(128)} %bitcast.35, f32[]{:T(128)} %bitcast.34, f32[]{:T(128)} %bitcast.33, f32[]{:T(128)} %bitcast.31), kind=kLoop, calls=%fused_computation.197 | loop fusion | flops 589824 | bytes 1245220 | tf_op jit(solution)/shard_map/stack | solution.py:96
  48.0 106.3 %all_to_all.5 = bf16[32,1,2,128,256]{4,3,2,1,0:T(8,128)(2,1)S(1)} all-to-all(bf16[32,1,2,128,256]{4,3,2,1,0:T(8,128)(2,1)S(1)} %stack.39), channel_id=1, replica_groups=mesh['tx'=4,'ty'=2,'ea'=32] {'ea'}, dimensions={0} | all-to-all | bytes 8388608 | tf_op jit(solution)/shard_map/all_to_all | solution.py:98
  154.6 3.2 collective-permute-start.4
  160.5 20.9 %collective-permute-done.4 = bf16[32,2,32,256]{3,2,1,0:T(8,128)(2,1)S(1)} collective-permute-done((bf16[32,2,32,256]{3,2,1,0:T(8,128)(2,1)S(1)}, bf16[32,2,32,256]{3,2,1,0:T(8,128)(2,1)S(1)}, u32[]{:S(2)}, u32[]{:S(2)}) %collective-permute-start.4) | collective-permute-done | bytes 1048608 | tf_op jit(solution)/shard_map/ppermute | solution.py:18
  185.2 4.2 %pad_maximum_fusion.1 = bf16[32,2,192,256]{3,2,1,0:T(8,128)(2,1)S(1)} fusion(bf16[32,2,32,256]{3,2,1,0:T(8,128)(2,1)S(1)} %collective-permute-done.5, bf16[32,2,128,256]{3,2,1,0:T(8,128)(2,1)S(1)} %bitcast.137, bf16[32,2,32,256]{3,2,1,0:T(8,128)(2,1)S(1)} %collective-permute-done.4), kind=kLoop, calls=%fused_computation.118 | loop fusion | flops 18874368 | bytes 12582912 | tf_op jit(solution)/shard_map/concatenate | solution.py:16
  189.4 3.2 fusion.141
  192.6 4.2 %copy.8 = bf16[32,2,192,32]{2,3,1,0:T(8,128)(2,1)} copy(bf16[32,2,192,32]{3,2,1,0:T(8,128)(2,1)} %get-tuple-element.176) | data formatting | bytes 1572864 | tf_op jit(solution)/shard_map/slice | solution.py:15
  199.0 3.0 copy.9
  203.5 16.3 %collective-permute-done.6 = bf16[32,2,192,32]{2,3,1,0:T(8,128)(2,1)} collective-permute-done((bf16[32,2,192,32]{2,3,1,0:T(8,128)(2,1)}, bf16[32,2,192,32]{2,3,1,0:T(8,128)(2,1)}, u32[]{:S(2)}, u32[]{:S(2)}) %collective-permute-start.6) | collective-permute-done | bytes 786464 | tf_op jit(solution)/shard_map/ppermute | solution.py:18
  219.9 3.4 copy.10
  223.3 4.7 %collective-permute-done.7 = bf16[32,2,192,32]{2,3,1,0:T(8,128)(2,1)} collective-permute-done((bf16[32,2,192,32]{2,3,1,0:T(8,128)(2,1)}, bf16[32,2,192,32]{2,3,1,0:T(8,128)(2,1)}, u32[]{:S(2)}, u32[]{:S(2)}) %collective-permute-start.7) | collective-permute-done | bytes 786464 | tf_op jit(solution)/shard_map/ppermute | solution.py:20
  227.9 3.9 %copy.11 = bf16[32,2,192,32]{3,2,1,0:T(8,128)(2,1)} copy(bf16[32,2,192,32]{2,3,1,0:T(8,128)(2,1)} %collective-permute-done.7) | data formatting | bytes 1572864 | tf_op jit(solution)/shard_map/ppermute | solution.py:20
  231.8 11.6 %pad_maximum_fusion = bf16[32,2,192,320]{3,2,1,0:T(8,128)(2,1)} fusion(bf16[32,2,192,32]{3,2,1,0:T(8,128)(2,1)} %copy.11, bf16[32,2,32,256]{3,2,1,0:T(8,128)(2,1)} %copy-done.2, bf16[32,2,128,256]{3,2,1,0:T(8,128)(2,1)} %bitcast.138, bf16[32,2,32,256]{3,2,1,0:T(8,128)(2,1)} %copy-done.1, bf16[32,2,192,32]{3,2,1,0:T(8,128)(2,1)S(1)} %copy.10), kind=kLoop, calls=%fused_computation.117 | loop fusion | flops 39321600 | bytes 15728640 | tf_op jit(solution)/shard_map/concatenate | solution.py:16
  243.4 105.6 %while.15 = (s32[]{:T(128)}, f32[6,2,128,256]{3,2,0,1:T(8,128)}, s32[6,2]{0,1:T(2,128)S(1)}, s32[32]{0:T(128)S(1)}, bf16[32,2,192,320]{3,2,1,0:T(8,128)(2,1)}, /*index=5*/s32[]{:T(128)}) while((s32[]{:T(128)}, f32[6,2,128,256]{3,2,0,1:T(8,128)}, s32[6,2]{0,1:T(2,128)S(1)}, s32[32]{0:T(128)S(1)}, bf16[32,2,192,320]{3,2,1,0:T(8,128)(2,1)}, ...), condition=%wide.region_2.3_spmd, body=%wide.region_1.2_spmd.sunk | while | flops 2396370688 | bytes 19467128 | solution.py:84
  246.5 7.6 %fusion.178 = bf16[32,2,128,320]{2,3,0,1:T(8,128)(2,1)S(1)} fusion(bf16[32,2,192,320]{3,2,1,0:T(8,128)(2,1)} %get-tuple-element.288, s32[32]{0:T(128)S(1)} %get-tuple-element.267, s32[128,192]{1,0:T(8,128)S(1)} %iota_subtract_fusion.5, bf16[32]{0:T(256)(128)(2,1)S(1)} %get-tuple-element.268, ...), kind=kOutput, calls=%fused_computation.19.clone.clone.clone.clone.clone.2.clone.1 | convolution fusion | flops 1022623744 | bytes 13205888 | tf_op jit(solution)/shard_map/while/body/eval_jaxpr/erp,eipk->eirk/dot_general | solution.py:79
  254.1 6.9 %fusion.179 = f32[6,2,128,256]{3,2,0,1:T(8,128)} fusion(f32[6,2,128,256]{3,2,0,1:T(8,128)} %get-tuple-element.279, s32[]{:T(128)} %get-tuple-element.278, s32[32]{0:T(128)S(1)} %get-tuple-element.260, s32[256,320]{0,1:T(8,128)S(1)} %iota_subtract_fusion.4, bf16[32]{0:T(256)(128)(2,1)S(1)} %get-tuple-element.263, ...), kind=kOutput, calls=%fused_computation.47.clone.3 | convolution fusion | flops 1373634560 | bytes 5833600 | tf_op jit(solution)/shard_map/while/body/eval_jaxpr/eirk,eck->irc/dot_general | solution.py:82
  264.1 7.6 %fusion.178 = bf16[32,2,128,320]{2,3,0,1:T(8,128)(2,1)S(1)} fusion(bf16[32,2,192,320]{3,2,1,0:T(8,128)(2,1)} %get-tuple-element.288, s32[32]{0:T(128)S(1)} %get-tuple-element.267, s32[128,192]{1,0:T(8,128)S(1)} %iota_subtract_fusion.5, bf16[32]{0:T(256)(128)(2,1)S(1)} %get-tuple-element.268, ...), kind=kOutput, calls=%fused_computation.19.clone.clone.clone.clone.clone.2.clone.1 | convolution fusion | flops 1022623744 | bytes 13205888 | tf_op jit(solution)/shard_map/while/body/eval_jaxpr/erp,eipk->eirk/dot_general | solution.py:79
  271.7 6.9 %fusion.179 = f32[6,2,128,256]{3,2,0,1:T(8,128)} fusion(f32[6,2,128,256]{3,2,0,1:T(8,128)} %get-tuple-element.279, s32[]{:T(128)} %get-tuple-element.278, s32[32]{0:T(128)S(1)} %get-tuple-element.260, s32[256,320]{0,1:T(8,128)S(1)} %iota_subtract_fusion.4, bf16[32]{0:T(256)(128)(2,1)S(1)} %get-tuple-element.263, ...), kind=kOutput, calls=%fused_computation.47.clone.3 | convolution fusion | flops 1373634560 | bytes 5833600 | tf_op jit(solution)/shard_map/while/body/eval_jaxpr/eirk,eck->irc/dot_general | solution.py:82
  281.7 7.6 %fusion.178 = bf16[32,2,128,320]{2,3,0,1:T(8,128)(2,1)S(1)} fusion(bf16[32,2,192,320]{3,2,1,0:T(8,128)(2,1)} %get-tuple-element.288, s32[32]{0:T(128)S(1)} %get-tuple-element.267, s32[128,192]{1,0:T(8,128)S(1)} %iota_subtract_fusion.5, bf16[32]{0:T(256)(128)(2,1)S(1)} %get-tuple-element.268, ...), kind=kOutput, calls=%fused_computation.19.clone.clone.clone.clone.clone.2.clone.1 | convolution fusion | flops 1022623744 | bytes 13205888 | tf_op jit(solution)/shard_map/while/body/eval_jaxpr/erp,eipk->eirk/dot_general | solution.py:79
  289.3 6.9 %fusion.179 = f32[6,2,128,256]{3,2,0,1:T(8,128)} fusion(f32[6,2,128,256]{3,2,0,1:T(8,128)} %get-tuple-element.279, s32[]{:T(128)} %get-tuple-element.278, s32[32]{0:T(128)S(1)} %get-tuple-element.260, s32[256,320]{0,1:T(8,128)S(1)} %iota_subtract_fusion.4, bf16[32]{0:T(256)(128)(2,1)S(1)} %get-tuple-element.263, ...), kind=kOutput, calls=%fused_computation.47.clone.3 | convolution fusion | flops 1373634560 | bytes 5833600 | tf_op jit(solution)/shard_map/while/body/eval_jaxpr/eirk,eck->irc/dot_general | solution.py:82
  299.3 7.6 %fusion.178 = bf16[32,2,128,320]{2,3,0,1:T(8,128)(2,1)S(1)} fusion(bf16[32,2,192,320]{3,2,1,0:T(8,128)(2,1)} %get-tuple-element.288, s32[32]{0:T(128)S(1)} %get-tuple-element.267, s32[128,192]{1,0:T(8,128)S(1)} %iota_subtract_fusion.5, bf16[32]{0:T(256)(128)(2,1)S(1)} %get-tuple-element.268, ...), kind=kOutput, calls=%fused_computation.19.clone.clone.clone.clone.clone.2.clone.1 | convolution fusion | flops 1022623744 | bytes 13205888 | tf_op jit(solution)/shard_map/while/body/eval_jaxpr/erp,eipk->eirk/dot_general | solution.py:79
  306.9 6.9 %fusion.179 = f32[6,2,128,256]{3,2,0,1:T(8,128)} fusion(f32[6,2,128,256]{3,2,0,1:T(8,128)} %get-tuple-element.279, s32[]{:T(128)} %get-tuple-element.278, s32[32]{0:T(128)S(1)} %get-tuple-element.260, s32[256,320]{0,1:T(8,128)S(1)} %iota_subtract_fusion.4, bf16[32]{0:T(256)(128)(2,1)S(1)} %get-tuple-element.263, ...), kind=kOutput, calls=%fused_computation.47.clone.3 | convolution fusion | flops 1373634560 | bytes 5833600 | tf_op jit(solution)/shard_map/while/body/eval_jaxpr/eirk,eck->irc/dot_general | solution.py:82
  316.8 7.6 %fusion.178 = bf16[32,2,128,320]{2,3,0,1:T(8,128)(2,1)S(1)} fusion(bf16[32,2,192,320]{3,2,1,0:T(8,128)(2,1)} %get-tuple-element.288, s32[32]{0:T(128)S(1)} %get-tuple-element.267, s32[128,192]{1,0:T(8,128)S(1)} %iota_subtract_fusion.5, bf16[32]{0:T(256)(128)(2,1)S(1)} %get-tuple-element.268, ...), kind=kOutput, calls=%fused_computation.19.clone.clone.clone.clone.clone.2.clone.1 | convolution fusion | flops 1022623744 | bytes 13205888 | tf_op jit(solution)/shard_map/while/body/eval_jaxpr/erp,eipk->eirk/dot_general | solution.py:79
  324.5 6.9 %fusion.179 = f32[6,2,128,256]{3,2,0,1:T(8,128)} fusion(f32[6,2,128,256]{3,2,0,1:T(8,128)} %get-tuple-element.279, s32[]{:T(128)} %get-tuple-element.278, s32[32]{0:T(128)S(1)} %get-tuple-element.260, s32[256,320]{0,1:T(8,128)S(1)} %iota_subtract_fusion.4, bf16[32]{0:T(256)(128)(2,1)S(1)} %get-tuple-element.263, ...), kind=kOutput, calls=%fused_computation.47.clone.3 | convolution fusion | flops 1373634560 | bytes 5833600 | tf_op jit(solution)/shard_map/while/body/eval_jaxpr/eirk,eck->irc/dot_general | solution.py:82
  334.5 7.6 %fusion.178 = bf16[32,2,128,320]{2,3,0,1:T(8,128)(2,1)S(1)} fusion(bf16[32,2,192,320]{3,2,1,0:T(8,128)(2,1)} %get-tuple-element.288, s32[32]{0:T(128)S(1)} %get-tuple-element.267, s32[128,192]{1,0:T(8,128)S(1)} %iota_subtract_fusion.5, bf16[32]{0:T(256)(128)(2,1)S(1)} %get-tuple-element.268, ...), kind=kOutput, calls=%fused_computation.19.clone.clone.clone.clone.clone.2.clone.1 | convolution fusion | flops 1022623744 | bytes 13205888 | tf_op jit(solution)/shard_map/while/body/eval_jaxpr/erp,eipk->eirk/dot_general | solution.py:79
  342.1 6.9 %fusion.179 = f32[6,2,128,256]{3,2,0,1:T(8,128)} fusion(f32[6,2,128,256]{3,2,0,1:T(8,128)} %get-tuple-element.279, s32[]{:T(128)} %get-tuple-element.278, s32[32]{0:T(128)S(1)} %get-tuple-element.260, s32[256,320]{0,1:T(8,128)S(1)} %iota_subtract_fusion.4, bf16[32]{0:T(256)(128)(2,1)S(1)} %get-tuple-element.263, ...), kind=kOutput, calls=%fused_computation.47.clone.3 | convolution fusion | flops 1373634560 | bytes 5833600 | tf_op jit(solution)/shard_map/while/body/eval_jaxpr/eirk,eck->irc/dot_general | solution.py:82
  (75 shorter events, 43.8 us)
Async XLA Ops:
  1.7 8.4 %collective-permute-start = (f32[2,1,4,256]{3,2,1,0:T(4,128)S(1)}, f32[2,1,4,256]{3,2,1,0:T(4,128)S(1)}, u32[]{:S(2)}, u32[]{:S(2)}) collective-permute-start(f32[2,1,4,256]{3,2,1,0:T(4,128)S(1)} %get-tuple-element.184), channel_id=1, source_target_pairs={{0,64},{64,128},{128,192},{1,65},{65,129},{129,193},{2,66},{66,130... | collective-permute-start | bytes 24584 | tf_op jit(solution)/shard_map/ppermute | solution.py:18
  5.2 5.5 %collective-permute-start.1 = (f32[2,1,4,256]{3,2,1,0:T(4,128)S(1)}, f32[2,1,4,256]{3,2,1,0:T(4,128)S(1)}, u32[]{:S(2)}, u32[]{:S(2)}) collective-permute-start(f32[2,1,4,256]{3,2,1,0:T(4,128)S(1)} %get-tuple-element.185), channel_id=1, source_target_pairs={{64,0},{128,64},{192,128},{65,1},{129,65},{193,129},{66,2},{130,66... | collective-permute-start | bytes 24584 | tf_op jit(solution)/shard_map/ppermute | solution.py:20
  11.8 6.4 %collective-permute-start.2 = (f32[2,1,136,4]{3,2,1,0:T(8,128)S(1)}, f32[2,1,136,4]{3,2,1,0:T(8,128)S(1)}, u32[]{:S(2)}, u32[]{:S(2)}) collective-permute-start(f32[2,1,136,4]{3,2,1,0:T(8,128)S(1)} %get-tuple-element.182), channel_id=1, source_target_pairs={{0,32},{1,33},{2,34},{3,35},{4,36},{5,37},{6,38},{7,39},{8,40},{9,... | collective-permute-start | bytes 13064 | tf_op jit(solution)/shard_map/ppermute | solution.py:18
  15.6 6.9 %collective-permute-start.3 = (f32[2,1,136,4]{3,2,1,0:T(8,128)S(1)}, f32[2,1,136,4]{3,2,1,0:T(8,128)S(1)}, u32[]{:S(2)}, u32[]{:S(2)}) collective-permute-start(f32[2,1,136,4]{3,2,1,0:T(8,128)S(1)} %get-tuple-element.183), channel_id=1, source_target_pairs={{32,0},{33,1},{34,2},{35,3},{36,4},{37,5},{38,6},{39,7},{40,8},{41... | collective-permute-start | bytes 13064 | tf_op jit(solution)/shard_map/ppermute | solution.py:20
  154.4 29.9 %copy-start = (bf16[32,1,2,128,256]{4,3,2,1,0:T(8,128)(2,1)}, bf16[32,1,2,128,256]{4,3,2,1,0:T(8,128)(2,1)S(1)}, u32[]{:S(2)}) copy-start(bf16[32,1,2,128,256]{4,3,2,1,0:T(8,128)(2,1)S(1)} %all_to_all.5) | copy-start | bytes 12582916
  154.6 26.8 %collective-permute-start.4 = (bf16[32,2,32,256]{3,2,1,0:T(8,128)(2,1)S(1)}, bf16[32,2,32,256]{3,2,1,0:T(8,128)(2,1)S(1)}, u32[]{:S(2)}, u32[]{:S(2)}) collective-permute-start(bf16[32,2,32,256]{3,2,1,0:T(8,128)(2,1)S(1)} %get-tuple-element.178), channel_id=1, source_target_pairs={{0,64},{64,128},{128,192},{1,65},{65,129},{129,193},{2,66},{66,130... | collective-permute-start | bytes 3145736 | tf_op jit(solution)/shard_map/ppermute | solution.py:18
  157.8 26.5 %collective-permute-start.5 = (bf16[32,2,32,256]{3,2,1,0:T(8,128)(2,1)S(1)}, bf16[32,2,32,256]{3,2,1,0:T(8,128)(2,1)S(1)}, u32[]{:S(2)}, u32[]{:S(2)}) collective-permute-start(bf16[32,2,32,256]{3,2,1,0:T(8,128)(2,1)S(1)} %get-tuple-element.179), channel_id=1, source_target_pairs={{64,0},{128,64},{192,128},{65,1},{129,65},{193,129},{66,2},{130,66... | collective-permute-start | bytes 3145736 | tf_op jit(solution)/shard_map/ppermute | solution.py:20
  181.3 2.9 copy-start.1
  184.3 1.0 copy-start.2
  196.8 23.1 %collective-permute-start.6 = (bf16[32,2,192,32]{2,3,1,0:T(8,128)(2,1)}, bf16[32,2,192,32]{2,3,1,0:T(8,128)(2,1)}, u32[]{:S(2)}, u32[]{:S(2)}) collective-permute-start(bf16[32,2,192,32]{2,3,1,0:T(8,128)(2,1)} %copy.8), channel_id=1, source_target_pairs={{0,32},{1,33},{2,34},{3,35},{4,36},{5,37},{6,38},{7,39},{8,40},{9,... | collective-permute-start | bytes 2359304 | tf_op jit(solution)/shard_map/ppermute | solution.py:18
  202.1 25.9 %collective-permute-start.7 = (bf16[32,2,192,32]{2,3,1,0:T(8,128)(2,1)}, bf16[32,2,192,32]{2,3,1,0:T(8,128)(2,1)}, u32[]{:S(2)}, u32[]{:S(2)}) collective-permute-start(bf16[32,2,192,32]{2,3,1,0:T(8,128)(2,1)} %copy.9), channel_id=1, source_target_pairs={{32,0},{33,1},{34,2},{35,3},{36,4},{37,5},{38,6},{39,7},{40,8},{41... | collective-permute-start | bytes 2359304 | tf_op jit(solution)/shard_map/ppermute | solution.py:20
  231.8 11.6 %copy-start.3 = (s32[32]{0:T(128)S(1)}, s32[32]{0:T(128)}, u32[]{:S(2)}) copy-start(s32[32]{0:T(128)} %param.10) | copy-start | bytes 388
  231.8 11.6 %copy-start.4 = (s32[6,2]{0,1:T(2,128)S(1)}, s32[6,2]{0,1:T(2,128)}, u32[]{:S(2)}) copy-start(s32[6,2]{0,1:T(2,128)} %param.11) | copy-start | bytes 148
